TPU v7x, 32 devices: a whole 2x2x4 slice. The times are simulated.
32 devices in a mesh: tm: 8 (over z, y), space: 4 (over x, core).
Axes of the slice: x: 2, y: 2, z: 4, core: 2. Of those that a mesh axis runs over, the one named last changes fastest.
Arguments:
- controls: bfloat16 [32, 64, 2048], P('tm', None, 'space'), may hold values from -4 to 4
- target: bfloat16 [64, 2048], P(None, 'space'), may hold values from -4 to 4
- state_in: float32 [8, 64, 2048], P('tm', None, 'space'), may hold values from -2.5 to 2.5
- adjoint_in: float32 [8, 64, 2048], P('tm', None, 'space'), may hold values from -5 to 5
- block_inverse: bfloat16 [64, 64, 2048], P(None, None, 'space'), may hold values from -1 to 1
- numbering: int32 [4, 512], P('space'), may hold values from 0 to 511, each once within a row
Outputs:
- new_controls: bfloat16 [32, 64, 2048], P('tm', None, 'space')
- next_state: float32 [8, 64, 2048], P('tm', None, 'space')
- next_adjoint: float32 [8, 64, 2048], P('tm', None, 'space')
- objective: float32 [], replicated
Inputs may be any that keep to these rules, and one draw needn't show every extreme that they name: `numbering`: each row names every structural element of its slab exactly once.
All inputs are finite; a program needn't handle non-finite values.
Results may differ from a plain program's by a relative error of at most 0.0085.
Values may be sent and summed in bfloat16 or wider, within the bound.
A program may use at most 128 MiB of HBM per device.

v0:
```python
import jax
import jax.numpy as jnp
from jax import lax
from jax.sharding import PartitionSpec as P

NSIDE = 4
EXY = 16
TIME_STEP = 0.1
PENALTY = 0.5
REGULAR = 0.1


def padded_2(cells, sides, width):
    for axis, dim in sides:
        count = lax.axis_size(axis)
        ends = count - 1
        head = lax.slice_in_dim(cells, 0, width, axis=dim)
        tail = lax.slice_in_dim(cells, cells.shape[dim] - width, cells.shape[dim], axis=dim)
        cells = jnp.concatenate(
            [
                lax.ppermute(tail, axis, [(i, (i + 1) % count) for i in range(ends)]),
                cells,
                lax.ppermute(head, axis, [((i + 1) % count, i) for i in range(ends)]),
            ],
            axis=dim,
        )
    return cells


def from_behind(shard, axis, by):
    length = lax.axis_size(axis)
    pairs = [(i, i + by) for i in range(length) if 0 <= i + by < length]
    return lax.ppermute(shard, axis, pairs)


def apply_block(blocks, right_side):
    return jnp.einsum("ije,je->ie", blocks, right_side, preferred_element_type=jnp.float32)


def apply_transpose(blocks, vector):
    return jnp.einsum("ije,ie->je", blocks, vector, preferred_element_type=jnp.float32)


def face_jumps(values, fetch, edges, node_side, elements):
    tensor = values.reshape(node_side, node_side, node_side, elements)
    last = node_side - 1
    lower_rim, upper_rim = edges(tensor[0], tensor[last])
    padded = padded_2(
        jnp.stack([lower_rim, upper_rim]).astype(jnp.bfloat16), (("space", 0),), 1
    ).astype(jnp.float32)
    rims = (padded[0], padded[3])
    west_jump = fetch("west", tensor[:, :, last, :], rims) - tensor[:, :, 0, :]
    east_jump = fetch("east", tensor[:, :, 0, :], rims) - tensor[:, :, last, :]
    south_jump = fetch("south", tensor[:, last, :, :], rims) - tensor[:, 0, :, :]
    north_jump = fetch("north", tensor[:, 0, :, :], rims) - tensor[:, last, :, :]
    lower_jump = fetch("lower", tensor[last], rims) - tensor[0]
    upper_jump = fetch("upper", tensor[0], rims) - tensor[last]
    total = jnp.zeros_like(tensor)
    total = total.at[:, :, 0, :].add(west_jump)
    total = total.at[:, :, last, :].add(east_jump)
    total = total.at[:, 0, :, :].add(south_jump)
    total = total.at[:, last, :, :].add(north_jump)
    total = total.at[0].add(lower_jump)
    total = total.at[last].add(upper_jump)
    return total.reshape(values.shape)


def per_device(controls, target, state_in, adjoint_in, block_inverse, numbering):
    steps_here = controls.shape[0]
    nodes = controls.shape[1]
    elements = controls.shape[2]
    node_side = NSIDE
    layer_cells = EXY * EXY
    layers = elements // layer_cells
    ordering = numbering[0]
    position = jnp.arange(elements, dtype=jnp.int32)
    inverse = jnp.zeros((elements,), jnp.int32).at[ordering].set(position)

    def arrange(values):
        return jnp.take(values, inverse, axis=-1)

    def restore(values):
        return jnp.take(values, ordering, axis=-1)

    def edges(lower_face, upper_face):
        return (lower_face[:, :, :layer_cells], upper_face[:, :, elements - layer_cells :])

    def fetch(face_name, traces, rims):
        shaped = traces.reshape(node_side, node_side, layers, EXY, EXY)
        if face_name == "west":
            moved = jnp.roll(shaped, 1, axis=4)
        elif face_name == "east":
            moved = jnp.roll(shaped, -1, axis=4)
        elif face_name == "south":
            moved = jnp.roll(shaped, 1, axis=3)
        elif face_name == "north":
            moved = jnp.roll(shaped, -1, axis=3)
        elif face_name == "lower":
            remote = rims[0].reshape(node_side, node_side, 1, EXY, EXY)
            moved = jnp.concatenate([remote, shaped[:, :, :-1]], axis=2)
        else:
            remote = rims[1].reshape(node_side, node_side, 1, EXY, EXY)
            moved = jnp.concatenate([shaped[:, :, 1:], remote], axis=2)
        return moved.reshape(traces.shape)

    def jumps_of(values):
        return face_jumps(values, fetch, edges, node_side, elements)

    blocks = arrange(block_inverse)
    goal = arrange(target).astype(jnp.float32)
    controls_here = arrange(controls)
    start_state = arrange(state_in[0])
    start_adjoint = arrange(adjoint_in[0])
    total_steps = steps_here * lax.axis_size("tm")
    first_step = lax.axis_index("tm") * steps_here
    history = [start_state]
    state = start_state
    misfit = jnp.float32(0.0)
    regular_sum = jnp.float32(0.0)
    right_side = None
    for index_k in range(steps_here):
        control_now = controls_here[index_k].astype(jnp.float32)
        right_side = (
            state
            + TIME_STEP * (state - state * state * state)
            + TIME_STEP * PENALTY * jumps_of(state)
            + TIME_STEP * control_now
        ).astype(jnp.bfloat16)
        state = apply_block(blocks, right_side)
        history.append(state)
        weight = (first_step + index_k + 1).astype(jnp.float32) / total_steps
        misfit = misfit + weight * jnp.sum((state - goal) ** 2)
        regular_sum = regular_sum + jnp.sum(control_now * control_now)
    local_cost = 0.5 * misfit + 0.5 * REGULAR * regular_sum
    end_weight = (first_step + steps_here).astype(jnp.float32) / total_steps
    adjoint = end_weight * (history[-1] - goal) + start_adjoint
    updated = [None] * steps_here
    carried = adjoint
    for index_k in reversed(range(steps_here)):
        pulled = apply_transpose(blocks, adjoint.astype(jnp.bfloat16))
        control_now = controls_here[index_k].astype(jnp.float32)
        updated[index_k] = (control_now - (TIME_STEP * pulled + REGULAR * control_now)).astype(
            jnp.bfloat16
        )
        before = history[index_k]
        carried = (
            pulled
            + TIME_STEP * (1.0 - 3.0 * before * before) * pulled
            + TIME_STEP * PENALTY * jumps_of(pulled)
        )
        if index_k > 0:
            weight = (first_step + index_k).astype(jnp.float32) / total_steps
            adjoint = weight * (before - goal) + carried
    new_controls = restore(jnp.stack(updated))
    objective = lax.psum(local_cost, ("tm", "space")) / (
        total_steps * nodes * elements * lax.axis_size("space")
    )
    moved_state = from_behind(history[-1].astype(jnp.bfloat16), "tm", 1).astype(jnp.float32)
    next_state = jnp.where(lax.axis_index("tm") == 0, state_in[0], restore(moved_state))[None]
    next_adjoint = from_behind(restore(carried), "tm", -1)[None]
    return (new_controls, next_state, next_adjoint, objective)


def solution(mesh):
    return jax.shard_map(
        per_device,
        mesh=mesh,
        in_specs=(
            P("tm", None, "space"),
            P(None, "space"),
            P("tm", None, "space"),
            P("tm", None, "space"),
            P(None, None, "space"),
            P("space", None),
        ),
        out_specs=(P("tm", None, "space"), P("tm", None, "space"), P("tm", None, "space"), P()),
        check_vma=False,
    )
```

profile of v0, /device:TPU:0, one launch (start us, length us, event | category | flops | bytes accessed | tf_op | source)
XLA Modules:
  0.0 264.8 jit_solution(15748085955801050513)
XLA Ops:
  1.4 2.4 scatter_custom_fusion
  6.1 2.4 collective-permute-start
  15.7 13.0 %copy.148 = bf16[64,64,512]{1,0,2:T(8,128)(2,1)} copy(bf16[64,64,512]{2,1,0:T(8,128)(2,1)} %param.110) | data formatting | bytes 8388608 | tf_op args[4]
  28.8 23.0 %gather_fusion = bf16[512,64,64]{2,1,0:T(8,128)(2,1)} fusion(bf16[64,64,512]{1,0,2:T(8,128)(2,1)} %copy.148, s32[1024]{0:T(1024)S(1)} %pad_clamp_fusion.1), kind=kCustom, calls=%fused_computation.6 | custom fusion | bytes 8390656 | tf_op jit(solution)/shard_map/jit(_take)/gather | solution.py:80
  55.7 8.3 %fusion = f32[512,64]{1,0:T(8,128)S(1)} fusion(f32[512,64]{1,0:T(8,128)S(1)} %copy.235, bf16[512,64,64]{2,1,0:T(8,128)(2,1)} %gather_fusion, pred[512]{0:T(512)(128)(4,1)S(1)} %compare_and_fusion.1), kind=kLoop, calls=%fused_computation.17 | loop fusion | flops 8355840 | bytes 4456960
  66.5 5.1 %collective-permute-start.2 = (bf16[1,4,4,256]{3,2,1,0:T(4,128)(2,1)S(1)}, bf16[1,4,4,256]{3,2,1,0:T(4,128)(2,1)S(1)}, u32[]{:S(2)}, u32[]{:S(2)}) collective-permute-start(bf16[1,4,4,256]{3,2,1,0:T(4,128)(2,1)S(1)} %slice_bitcast_fusion.17), channel_id=1, source_target_pairs={{0,1},{1,2},{2,3},{4,5},{5,6},{6,7},{8,9},{9,10},{10,11},{12,13},{... | collective-permute-start | bytes 24584 | tf_op jit(solution)/shard_map/ppermute | solution.py:21
  73.5 2.4 collective-permute-done.3
  76.9 8.1 %fusion.1 = f32[512,64]{1,0:T(8,128)S(1)} fusion(f32[512,64]{1,0:T(8,128)S(1)} %copy.236, bf16[512,64,64]{2,1,0:T(8,128)(2,1)} %gather_fusion, pred[512]{0:T(512)(128)(4,1)S(1)} %compare_and_fusion.1), kind=kLoop, calls=%fused_computation.18 | loop fusion | flops 8355840 | bytes 4456960
  87.5 4.3 %collective-permute-start.4 = (bf16[1,4,4,256]{3,2,1,0:T(4,128)(2,1)S(1)}, bf16[1,4,4,256]{3,2,1,0:T(4,128)(2,1)S(1)}, u32[]{:S(2)}, u32[]{:S(2)}) collective-permute-start(bf16[1,4,4,256]{3,2,1,0:T(4,128)(2,1)S(1)} %slice_bitcast_fusion.15), channel_id=1, source_target_pairs={{0,1},{1,2},{2,3},{4,5},{5,6},{6,7},{8,9},{9,10},{10,11},{12,13},{... | collective-permute-start | bytes 24584 | tf_op jit(solution)/shard_map/ppermute | solution.py:21
  95.8 8.5 %fusion.2 = f32[512,64]{1,0:T(8,128)S(1)} fusion(f32[512,64]{1,0:T(8,128)S(1)} %copy.237, bf16[512,64,64]{2,1,0:T(8,128)(2,1)} %gather_fusion, pred[512]{0:T(512)(128)(4,1)S(1)} %compare_and_fusion.1), kind=kLoop, calls=%fused_computation.19 | loop fusion | flops 8355840 | bytes 4456960
  106.8 3.8 %collective-permute-start.6 = (bf16[1,4,4,256]{3,2,1,0:T(4,128)(2,1)S(1)}, bf16[1,4,4,256]{3,2,1,0:T(4,128)(2,1)S(1)}, u32[]{:S(2)}, u32[]{:S(2)}) collective-permute-start(bf16[1,4,4,256]{3,2,1,0:T(4,128)(2,1)S(1)} %slice_bitcast_fusion.13), channel_id=1, source_target_pairs={{0,1},{1,2},{2,3},{4,5},{5,6},{6,7},{8,9},{9,10},{10,11},{12,13},{... | collective-permute-start | bytes 24584 | tf_op jit(solution)/shard_map/ppermute | solution.py:21
  114.7 8.1 %fusion.3 = f32[512,64]{1,0:T(8,128)S(1)} fusion(f32[512,64]{1,0:T(8,128)S(1)} %copy.238, bf16[512,64,64]{2,1,0:T(8,128)(2,1)} %gather_fusion, pred[512]{0:T(512)(128)(4,1)S(1)} %compare_and_fusion.1), kind=kLoop, calls=%fused_computation.20 | loop fusion | flops 8355840 | bytes 4456960
  123.1 8.2 %fusion.4 = f32[512,64]{1,0:T(8,128)S(1)} fusion(f32[512,64]{1,0:T(8,128)S(1)} %copy.239, bf16[512,64,64]{2,1,0:T(8,128)(2,1)} %gather_fusion, pred[512]{0:T(512)(128)(4,1)S(1)} %compare_and_fusion.1), kind=kLoop, calls=%fused_computation.21 | loop fusion | flops 8355840 | bytes 4456960
  134.0 3.8 %collective-permute-start.8 = (bf16[1,4,4,256]{3,2,1,0:T(4,128)(2,1)S(1)}, bf16[1,4,4,256]{3,2,1,0:T(4,128)(2,1)S(1)}, u32[]{:S(2)}, u32[]{:S(2)}) collective-permute-start(bf16[1,4,4,256]{3,2,1,0:T(4,128)(2,1)S(1)} %slice_bitcast_fusion.11), channel_id=1, source_target_pairs={{0,1},{1,2},{2,3},{4,5},{5,6},{6,7},{8,9},{9,10},{10,11},{12,13},{... | collective-permute-start | bytes 24584 | tf_op jit(solution)/shard_map/ppermute | solution.py:21
  139.4 3.4 %collective-permute-start.14 = (bf16[64,512]{1,0:T(8,128)(2,1)S(1)}, bf16[64,512]{1,0:T(8,128)(2,1)S(1)}, u32[]{:S(2)}, u32[]{:S(2)}) collective-permute-start(bf16[64,512]{1,0:T(8,128)(2,1)S(1)} %bitcast_convert_fusion), channel_id=1, source_target_pairs={{0,4},{4,8},{8,12},{12,16},{16,20},{20,24},{24,28},{1,5},{5,9},{9,... | collective-permute-start | bytes 196616 | tf_op jit(solution)/shard_map/ppermute | solution.py:33
  144.0 8.4 %fusion.5 = f32[512,64]{1,0:T(8,128)S(1)} fusion(f32[512,64]{1,0:T(8,128)S(1)} %copy.240, bf16[512,64,64]{2,1,0:T(8,128)(2,1)} %gather_fusion, pred[512]{0:T(512)(128)(4,1)S(1)} %compare_and_fusion.1), kind=kLoop, calls=%fused_computation.22 | loop fusion | flops 8355840 | bytes 4456960
  154.8 2.8 %collective-permute-start.10 = (bf16[1,4,4,256]{3,2,1,0:T(4,128)(2,1)S(1)}, bf16[1,4,4,256]{3,2,1,0:T(4,128)(2,1)S(1)}, u32[]{:S(2)}, u32[]{:S(2)}) collective-permute-start(bf16[1,4,4,256]{3,2,1,0:T(4,128)(2,1)S(1)} %slice_bitcast_fusion.9), channel_id=1, source_target_pairs={{0,1},{1,2},{2,3},{4,5},{5,6},{6,7},{8,9},{9,10},{10,11},{12,13},{... | collective-permute-start | bytes 24584 | tf_op jit(solution)/shard_map/ppermute | solution.py:21
  159.5 2.2 collective-permute-done.11
  163.3 8.2 %fusion.6 = f32[512,64]{1,0:T(8,128)S(1)} fusion(f32[512,64]{1,0:T(8,128)S(1)} %copy.241, bf16[512,64,64]{2,1,0:T(8,128)(2,1)} %gather_fusion, pred[512]{0:T(512)(128)(4,1)S(1)} %compare_and_fusion.1), kind=kLoop, calls=%fused_computation.23 | loop fusion | flops 8355840 | bytes 4456960
  174.0 4.3 %collective-permute-start.12 = (bf16[1,4,4,256]{3,2,1,0:T(4,128)(2,1)S(1)}, bf16[1,4,4,256]{3,2,1,0:T(4,128)(2,1)S(1)}, u32[]{:S(2)}, u32[]{:S(2)}) collective-permute-start(bf16[1,4,4,256]{3,2,1,0:T(4,128)(2,1)S(1)} %slice_bitcast_fusion.7), channel_id=1, source_target_pairs={{0,1},{1,2},{2,3},{4,5},{5,6},{6,7},{8,9},{9,10},{10,11},{12,13},{... | collective-permute-start | bytes 24584 | tf_op jit(solution)/shard_map/ppermute | solution.py:21
  183.8 8.2 %fusion.7 = f32[512,64]{1,0:T(8,128)S(1)} fusion(f32[512,64]{1,0:T(8,128)S(1)} %copy.242, bf16[512,64,64]{2,1,0:T(8,128)(2,1)} %gather_fusion, pred[512]{0:T(512)(128)(4,1)S(1)} %compare_and_fusion.1), kind=kLoop, calls=%fused_computation.24 | loop fusion | flops 8355840 | bytes 4456960
  194.5 3.0 %collective-permute-start.15 = (bf16[1,4,4,256]{3,2,1,0:T(4,128)(2,1)S(1)}, bf16[1,4,4,256]{3,2,1,0:T(4,128)(2,1)S(1)}, u32[]{:S(2)}, u32[]{:S(2)}) collective-permute-start(bf16[1,4,4,256]{3,2,1,0:T(4,128)(2,1)S(1)} %slice_bitcast_fusion.5), channel_id=1, source_target_pairs={{0,1},{1,2},{2,3},{4,5},{5,6},{6,7},{8,9},{9,10},{10,11},{12,13},{... | collective-permute-start | bytes 24584 | tf_op jit(solution)/shard_map/ppermute | solution.py:21
  211.0 41.3 %psum.7 = f32[]{:T(128)} all-reduce(f32[]{:T(128)S(6)} %add.563), channel_id=1, replica_groups=mesh['tm'=8,'space'=4] {'tm','space'}, use_global_device_ids=true, to_apply=%region_9.12 | all-reduce | flops 1 | bytes 8 | tf_op jit(solution)/shard_map/psum | solution.py:155
  257.3 5.3 %collective-permute-done.17 = f32[64,512]{0,1:T(8,128)S(1)} collective-permute-done((f32[64,512]{0,1:T(8,128)S(1)}, f32[64,512]{0,1:T(8,128)S(1)}, u32[]{:S(2)}, u32[]{:S(2)}) %collective-permute-start.17) | collective-permute-done | bytes 131104 | tf_op jit(solution)/shard_map/ppermute | solution.py:33
  (477 shorter events, 64.8 us)
Async XLA Ops:
  0.6 11.7 %copy-start.3 = (s32[1,512]{1,0:T(1,128)S(1)}, s32[1,512]{1,0:T(1,128)}, u32[]{:S(2)}) copy-start(s32[1,512]{1,0:T(1,128)} %param.111) | copy-start | bytes 6148
  0.6 11.9 %copy-start = (bf16[4,64,512]{2,1,0:T(8,128)(2,1)S(1)}, bf16[4,64,512]{2,1,0:T(8,128)(2,1)}, u32[]{:S(2)}) copy-start(bf16[4,64,512]{2,1,0:T(8,128)(2,1)} %param.106) | copy-start | bytes 786436
  6.1 48.6 %collective-permute-start = (bf16[1,4,4,256]{3,2,1,0:T(4,128)(2,1)S(1)}, bf16[1,4,4,256]{3,2,1,0:T(4,128)(2,1)S(1)}, u32[]{:S(2)}, u32[]{:S(2)}) collective-permute-start(bf16[1,4,4,256]{3,2,1,0:T(4,128)(2,1)S(1)} %slice_bitcast_fusion.19), channel_id=1, source_target_pairs={{0,1},{1,2},{2,3},{4,5},{5,6},{6,7},{8,9},{9,10},{10,11},{12,13},{... | collective-permute-start | bytes 24584 | tf_op jit(solution)/shard_map/ppermute | solution.py:21
  8.6 46.2 %collective-permute-start.1 = (bf16[1,4,4,256]{3,2,1,0:T(4,128)(2,1)S(1)}, bf16[1,4,4,256]{3,2,1,0:T(4,128)(2,1)S(1)}, u32[]{:S(2)}, u32[]{:S(2)}) collective-permute-start(bf16[1,4,4,256]{3,2,1,0:T(4,128)(2,1)S(1)} %slice_bitcast_fusion.18), channel_id=1, source_target_pairs={{1,0},{2,1},{3,2},{5,4},{6,5},{7,6},{9,8},{10,9},{11,10},{13,12},{... | collective-permute-start | bytes 24584 | tf_op jit(solution)/shard_map/ppermute | solution.py:23
  15.7 36.1 %copy-start.2 = (bf16[64,512]{1,0:T(8,128)(2,1)S(1)}, bf16[64,512]{1,0:T(8,128)(2,1)}, u32[]{:S(2)}) copy-start(bf16[64,512]{1,0:T(8,128)(2,1)} %param.107) | copy-start | bytes 196612
  15.7 37.7 %copy-start.1 = (f32[1,64,512]{2,1,0:T(8,128)S(1)}, f32[1,64,512]{2,1,0:T(8,128)}, u32[]{:S(2)}) copy-start(f32[1,64,512]{2,1,0:T(8,128)} %param.109) | copy-start | bytes 393220
  66.5 7.1 %collective-permute-start.2 = (bf16[1,4,4,256]{3,2,1,0:T(4,128)(2,1)S(1)}, bf16[1,4,4,256]{3,2,1,0:T(4,128)(2,1)S(1)}, u32[]{:S(2)}, u32[]{:S(2)}) collective-permute-start(bf16[1,4,4,256]{3,2,1,0:T(4,128)(2,1)S(1)} %slice_bitcast_fusion.17), channel_id=1, source_target_pairs={{0,1},{1,2},{2,3},{4,5},{5,6},{6,7},{8,9},{9,10},{10,11},{12,13},{... | collective-permute-start | bytes 24584 | tf_op jit(solution)/shard_map/ppermute | solution.py:21
  71.6 4.3 %collective-permute-start.3 = (bf16[1,4,4,256]{3,2,1,0:T(4,128)(2,1)S(1)}, bf16[1,4,4,256]{3,2,1,0:T(4,128)(2,1)S(1)}, u32[]{:S(2)}, u32[]{:S(2)}) collective-permute-start(bf16[1,4,4,256]{3,2,1,0:T(4,128)(2,1)S(1)} %slice_bitcast_fusion.16), channel_id=1, source_target_pairs={{1,0},{2,1},{3,2},{5,4},{6,5},{7,6},{9,8},{10,9},{11,10},{13,12},{... | collective-permute-start | bytes 24584 | tf_op jit(solution)/shard_map/ppermute | solution.py:23
  87.5 6.2 %collective-permute-start.4 = (bf16[1,4,4,256]{3,2,1,0:T(4,128)(2,1)S(1)}, bf16[1,4,4,256]{3,2,1,0:T(4,128)(2,1)S(1)}, u32[]{:S(2)}, u32[]{:S(2)}) collective-permute-start(bf16[1,4,4,256]{3,2,1,0:T(4,128)(2,1)S(1)} %slice_bitcast_fusion.15), channel_id=1, source_target_pairs={{0,1},{1,2},{2,3},{4,5},{5,6},{6,7},{8,9},{9,10},{10,11},{12,13},{... | collective-permute-start | bytes 24584 | tf_op jit(solution)/shard_map/ppermute | solution.py:21
  91.8 3.1 %collective-permute-start.5 = (bf16[1,4,4,256]{3,2,1,0:T(4,128)(2,1)S(1)}, bf16[1,4,4,256]{3,2,1,0:T(4,128)(2,1)S(1)}, u32[]{:S(2)}, u32[]{:S(2)}) collective-permute-start(bf16[1,4,4,256]{3,2,1,0:T(4,128)(2,1)S(1)} %slice_bitcast_fusion.14), channel_id=1, source_target_pairs={{1,0},{2,1},{3,2},{5,4},{6,5},{7,6},{9,8},{10,9},{11,10},{13,12},{... | collective-permute-start | bytes 24584 | tf_op jit(solution)/shard_map/ppermute | solution.py:23
  106.8 5.8 %collective-permute-start.6 = (bf16[1,4,4,256]{3,2,1,0:T(4,128)(2,1)S(1)}, bf16[1,4,4,256]{3,2,1,0:T(4,128)(2,1)S(1)}, u32[]{:S(2)}, u32[]{:S(2)}) collective-permute-start(bf16[1,4,4,256]{3,2,1,0:T(4,128)(2,1)S(1)} %slice_bitcast_fusion.13), channel_id=1, source_target_pairs={{0,1},{1,2},{2,3},{4,5},{5,6},{6,7},{8,9},{9,10},{10,11},{12,13},{... | collective-permute-start | bytes 24584 | tf_op jit(solution)/shard_map/ppermute | solution.py:21
  110.7 3.1 %collective-permute-start.7 = (bf16[1,4,4,256]{3,2,1,0:T(4,128)(2,1)S(1)}, bf16[1,4,4,256]{3,2,1,0:T(4,128)(2,1)S(1)}, u32[]{:S(2)}, u32[]{:S(2)}) collective-permute-start(bf16[1,4,4,256]{3,2,1,0:T(4,128)(2,1)S(1)} %slice_bitcast_fusion.12), channel_id=1, source_target_pairs={{1,0},{2,1},{3,2},{5,4},{6,5},{7,6},{9,8},{10,9},{11,10},{13,12},{... | collective-permute-start | bytes 24584 | tf_op jit(solution)/shard_map/ppermute | solution.py:23
  134.0 9.0 %collective-permute-start.8 = (bf16[1,4,4,256]{3,2,1,0:T(4,128)(2,1)S(1)}, bf16[1,4,4,256]{3,2,1,0:T(4,128)(2,1)S(1)}, u32[]{:S(2)}, u32[]{:S(2)}) collective-permute-start(bf16[1,4,4,256]{3,2,1,0:T(4,128)(2,1)S(1)} %slice_bitcast_fusion.11), channel_id=1, source_target_pairs={{0,1},{1,2},{2,3},{4,5},{5,6},{6,7},{8,9},{9,10},{10,11},{12,13},{... | collective-permute-start | bytes 24584 | tf_op jit(solution)/shard_map/ppermute | solution.py:21
  137.8 5.2 %collective-permute-start.9 = (bf16[1,4,4,256]{3,2,1,0:T(4,128)(2,1)S(1)}, bf16[1,4,4,256]{3,2,1,0:T(4,128)(2,1)S(1)}, u32[]{:S(2)}, u32[]{:S(2)}) collective-permute-start(bf16[1,4,4,256]{3,2,1,0:T(4,128)(2,1)S(1)} %slice_bitcast_fusion.10), channel_id=1, source_target_pairs={{1,0},{2,1},{3,2},{5,4},{6,5},{7,6},{9,8},{10,9},{11,10},{13,12},{... | collective-permute-start | bytes 24584 | tf_op jit(solution)/shard_map/ppermute | solution.py:23
  139.4 115.9 %collective-permute-start.14 = (bf16[64,512]{1,0:T(8,128)(2,1)S(1)}, bf16[64,512]{1,0:T(8,128)(2,1)S(1)}, u32[]{:S(2)}, u32[]{:S(2)}) collective-permute-start(bf16[64,512]{1,0:T(8,128)(2,1)S(1)} %bitcast_convert_fusion), channel_id=1, source_target_pairs={{0,4},{4,8},{8,12},{12,16},{16,20},{20,24},{24,28},{1,5},{5,9},{9,... | collective-permute-start | bytes 196616 | tf_op jit(solution)/shard_map/ppermute | solution.py:33
  154.8 4.7 %collective-permute-start.10 = (bf16[1,4,4,256]{3,2,1,0:T(4,128)(2,1)S(1)}, bf16[1,4,4,256]{3,2,1,0:T(4,128)(2,1)S(1)}, u32[]{:S(2)}, u32[]{:S(2)}) collective-permute-start(bf16[1,4,4,256]{3,2,1,0:T(4,128)(2,1)S(1)} %slice_bitcast_fusion.9), channel_id=1, source_target_pairs={{0,1},{1,2},{2,3},{4,5},{5,6},{6,7},{8,9},{9,10},{10,11},{12,13},{... | collective-permute-start | bytes 24584 | tf_op jit(solution)/shard_map/ppermute | solution.py:21
  157.6 4.1 %collective-permute-start.11 = (bf16[1,4,4,256]{3,2,1,0:T(4,128)(2,1)S(1)}, bf16[1,4,4,256]{3,2,1,0:T(4,128)(2,1)S(1)}, u32[]{:S(2)}, u32[]{:S(2)}) collective-permute-start(bf16[1,4,4,256]{3,2,1,0:T(4,128)(2,1)S(1)} %slice_bitcast_fusion.8), channel_id=1, source_target_pairs={{1,0},{2,1},{3,2},{5,4},{6,5},{7,6},{9,8},{10,9},{11,10},{13,12},{... | collective-permute-start | bytes 24584 | tf_op jit(solution)/shard_map/ppermute | solution.py:23
  174.0 8.8 %collective-permute-start.12 = (bf16[1,4,4,256]{3,2,1,0:T(4,128)(2,1)S(1)}, bf16[1,4,4,256]{3,2,1,0:T(4,128)(2,1)S(1)}, u32[]{:S(2)}, u32[]{:S(2)}) collective-permute-start(bf16[1,4,4,256]{3,2,1,0:T(4,128)(2,1)S(1)} %slice_bitcast_fusion.7), channel_id=1, source_target_pairs={{0,1},{1,2},{2,3},{4,5},{5,6},{6,7},{8,9},{9,10},{10,11},{12,13},{... | collective-permute-start | bytes 24584 | tf_op jit(solution)/shard_map/ppermute | solution.py:21
  178.3 4.5 %collective-permute-start.13 = (bf16[1,4,4,256]{3,2,1,0:T(4,128)(2,1)S(1)}, bf16[1,4,4,256]{3,2,1,0:T(4,128)(2,1)S(1)}, u32[]{:S(2)}, u32[]{:S(2)}) collective-permute-start(bf16[1,4,4,256]{3,2,1,0:T(4,128)(2,1)S(1)} %slice_bitcast_fusion.6), channel_id=1, source_target_pairs={{1,0},{2,1},{3,2},{5,4},{6,5},{7,6},{9,8},{10,9},{11,10},{13,12},{... | collective-permute-start | bytes 24584 | tf_op jit(solution)/shard_map/ppermute | solution.py:23
  194.5 5.2 %collective-permute-start.15 = (bf16[1,4,4,256]{3,2,1,0:T(4,128)(2,1)S(1)}, bf16[1,4,4,256]{3,2,1,0:T(4,128)(2,1)S(1)}, u32[]{:S(2)}, u32[]{:S(2)}) collective-permute-start(bf16[1,4,4,256]{3,2,1,0:T(4,128)(2,1)S(1)} %slice_bitcast_fusion.5), channel_id=1, source_target_pairs={{0,1},{1,2},{2,3},{4,5},{5,6},{6,7},{8,9},{9,10},{10,11},{12,13},{... | collective-permute-start | bytes 24584 | tf_op jit(solution)/shard_map/ppermute | solution.py:21
  197.6 3.8 %collective-permute-start.16 = (bf16[1,4,4,256]{3,2,1,0:T(4,128)(2,1)S(1)}, bf16[1,4,4,256]{3,2,1,0:T(4,128)(2,1)S(1)}, u32[]{:S(2)}, u32[]{:S(2)}) collective-permute-start(bf16[1,4,4,256]{3,2,1,0:T(4,128)(2,1)S(1)} %slice_bitcast_fusion.4), channel_id=1, source_target_pairs={{1,0},{2,1},{3,2},{5,4},{6,5},{7,6},{9,8},{10,9},{11,10},{13,12},{... | collective-permute-start | bytes 24584 | tf_op jit(solution)/shard_map/ppermute | solution.py:23
  253.3 9.3 %collective-permute-start.17 = (f32[64,512]{0,1:T(8,128)S(1)}, f32[64,512]{0,1:T(8,128)S(1)}, u32[]{:S(2)}, u32[]{:S(2)}) collective-permute-start(f32[64,512]{0,1:T(8,128)S(1)} %select_bitcast_fusion.1), channel_id=1, source_target_pairs={{4,0},{8,4},{12,8},{16,12},{20,16},{24,20},{28,24},{5,1},{9,5},{13... | collective-permute-start | bytes 393224 | tf_op jit(solution)/shard_map/ppermute | solution.py:33
where the time goes:
time: 269 us; the launch traced here: 265 us
  local copies, waits for them, and re-layouts  77.5 us (29%)
  other arithmetic  76 us (28%)
  starting transfers between devices  44.9 us (17%)
  blocking collectives  41.3 us (15%)
  waiting for transfers between devices  14 us (5%)
  between operations  11 us (4%)
    unnamed x15, other arithmetic  66.5 us
    psum x1, blocking collectives, per_device(): lax.psum(local_cost, ('tm', 'space'))  41.3 us
    ppermute x8, starting transfers between devices, padded_2(): lax.ppermute(tail, axis, [(i, (i + 1) % count) for i in range(ends)])  29.6 us
    gather x9, local copies, waits for them, and re-layouts, arrange(): return jnp.take(values, inverse, axis=-1)  29.1 us
    unnamed x24, local copies, waits for them, and re-layouts  18.2 us
    ppermute x8, starting transfers between devices, padded_2(): lax.ppermute(head, axis, [((i + 1) % count, i) for i in range(ends)])  10.5 us
    ppermute x8, waiting for transfers between devices, padded_2(): lax.ppermute(head, axis, [((i + 1) % count, i) for i in range(ends)])  8.72 us
    reshape x48, local copies, waits for them, and re-layouts, fetch(): return moved.reshape(traces.shape)  7.46 us
  transfers between devices with their start and end apart: 18, of which 6 were waited for; matrix products, arithmetic and copies ran while one was open for 35% of the time, Pallas kernels for 0%

commit v1 on v0

--- a/solution.py
+++ b/solution.py
@@ -8,6 +8,11 @@
 TIME_STEP = 0.1
 PENALTY = 0.5
 REGULAR = 0.1
+
+
+def summed_here(x, mesh_axis):
+    shards = lax.all_gather(x, mesh_axis)
+    return jnp.sum(shards, axis=0)
 
 
 def padded_2(cells, sides, width):
@@ -152,7 +157,7 @@
             weight = (first_step + index_k).astype(jnp.float32) / total_steps
             adjoint = weight * (before - goal) + carried
     new_controls = restore(jnp.stack(updated))
-    objective = lax.psum(local_cost, ("tm", "space")) / (
+    objective = summed_here(local_cost, ("tm", "space")) / (
         total_steps * nodes * elements * lax.axis_size("space")
     )
     moved_state = from_behind(history[-1].astype(jnp.bfloat16), "tm", 1).astype(jnp.float32)

time: 269 us -> 269 us (level)
    unnamed x0 -> x1, blocking collectives: none -> 41.3 us
    psum x1 -> x0, blocking collectives: 41.3 us -> none  [per_device(): lax.psum(local_cost, ('tm', 'space'))]
    unnamed x24 -> x26, local copies, waits for them, and re-layouts: 18.2 us -> 18.3 us
where the time goes in v1:
time: 269 us; the launch traced here: 265 us
  local copies, waits for them, and re-layouts  77.7 us (29%)
  other arithmetic  76.6 us (28%)
  starting transfers between devices  44.9 us (17%)
  blocking collectives  41.3 us (15%)
  waiting for transfers between devices  13.8 us (5%)
  between operations  11 us (4%)
    unnamed x15, other arithmetic  66.5 us
    unnamed x1, blocking collectives  41.3 us
    ppermute x8, starting transfers between devices, padded_2(): lax.ppermute(tail, axis, [(i, (i + 1) % count) for i in range(ends)])  29.6 us
    gather x9, local copies, waits for them, and re-layouts, arrange(): return jnp.take(values, inverse, axis=-1)  29.1 us
    unnamed x26, local copies, waits for them, and re-layouts  18.3 us
    ppermute x8, starting transfers between devices, padded_2(): lax.ppermute(head, axis, [((i + 1) % count, i) for i in range(ends)])  10.5 us
    ppermute x8, waiting for transfers between devices, padded_2(): lax.ppermute(head, axis, [((i + 1) % count, i) for i in range(ends)])  8.72 us
    reshape x48, local copies, waits for them, and re-layouts, fetch(): return moved.reshape(traces.shape)  7.46 us
  transfers between devices with their start and end apart: 18, of which 6 were waited for; matrix products, arithmetic and copies ran while one was open for 35% of the time, Pallas kernels for 0%

profile of v1, /device:TPU:0, one launch (start us, length us, event | category | flops | bytes accessed | tf_op | source)
XLA Modules:
  0.0 265.3 jit_solution(9593343008857703814)
XLA Ops:
  1.4 2.4 scatter_custom_fusion
  6.1 2.4 collective-permute-start
  15.7 13.0 %copy.148 = bf16[64,64,512]{1,0,2:T(8,128)(2,1)} copy(bf16[64,64,512]{2,1,0:T(8,128)(2,1)} %param.110) | data formatting | bytes 8388608 | tf_op args[4]
  28.8 23.0 %gather_fusion = bf16[512,64,64]{2,1,0:T(8,128)(2,1)} fusion(bf16[64,64,512]{1,0,2:T(8,128)(2,1)} %copy.148, s32[1024]{0:T(1024)S(1)} %pad_clamp_fusion.1), kind=kCustom, calls=%fused_computation.6 | custom fusion | bytes 8390656 | tf_op jit(solution)/shard_map/jit(_take)/gather | solution.py:85
  55.7 8.3 %fusion = f32[512,64]{1,0:T(8,128)S(1)} fusion(f32[512,64]{1,0:T(8,128)S(1)} %copy.235, bf16[512,64,64]{2,1,0:T(8,128)(2,1)} %gather_fusion, pred[512]{0:T(512)(128)(4,1)S(1)} %compare_and_fusion.1), kind=kLoop, calls=%fused_computation.17 | loop fusion | flops 8355840 | bytes 4456960
  66.5 5.1 %collective-permute-start.2 = (bf16[1,4,4,256]{3,2,1,0:T(4,128)(2,1)S(1)}, bf16[1,4,4,256]{3,2,1,0:T(4,128)(2,1)S(1)}, u32[]{:S(2)}, u32[]{:S(2)}) collective-permute-start(bf16[1,4,4,256]{3,2,1,0:T(4,128)(2,1)S(1)} %slice_bitcast_fusion.17), channel_id=1, source_target_pairs={{0,1},{1,2},{2,3},{4,5},{5,6},{6,7},{8,9},{9,10},{10,11},{12,13},{... | collective-permute-start | bytes 24584 | tf_op jit(solution)/shard_map/ppermute | solution.py:26
  73.6 2.4 collective-permute-done.3
  76.9 8.1 %fusion.1 = f32[512,64]{1,0:T(8,128)S(1)} fusion(f32[512,64]{1,0:T(8,128)S(1)} %copy.236, bf16[512,64,64]{2,1,0:T(8,128)(2,1)} %gather_fusion, pred[512]{0:T(512)(128)(4,1)S(1)} %compare_and_fusion.1), kind=kLoop, calls=%fused_computation.18 | loop fusion | flops 8355840 | bytes 4456960
  87.5 4.3 %collective-permute-start.4 = (bf16[1,4,4,256]{3,2,1,0:T(4,128)(2,1)S(1)}, bf16[1,4,4,256]{3,2,1,0:T(4,128)(2,1)S(1)}, u32[]{:S(2)}, u32[]{:S(2)}) collective-permute-start(bf16[1,4,4,256]{3,2,1,0:T(4,128)(2,1)S(1)} %slice_bitcast_fusion.15), channel_id=1, source_target_pairs={{0,1},{1,2},{2,3},{4,5},{5,6},{6,7},{8,9},{9,10},{10,11},{12,13},{... | collective-permute-start | bytes 24584 | tf_op jit(solution)/shard_map/ppermute | solution.py:26
  95.8 8.5 %fusion.2 = f32[512,64]{1,0:T(8,128)S(1)} fusion(f32[512,64]{1,0:T(8,128)S(1)} %copy.237, bf16[512,64,64]{2,1,0:T(8,128)(2,1)} %gather_fusion, pred[512]{0:T(512)(128)(4,1)S(1)} %compare_and_fusion.1), kind=kLoop, calls=%fused_computation.19 | loop fusion | flops 8355840 | bytes 4456960
  106.8 3.8 %collective-permute-start.6 = (bf16[1,4,4,256]{3,2,1,0:T(4,128)(2,1)S(1)}, bf16[1,4,4,256]{3,2,1,0:T(4,128)(2,1)S(1)}, u32[]{:S(2)}, u32[]{:S(2)}) collective-permute-start(bf16[1,4,4,256]{3,2,1,0:T(4,128)(2,1)S(1)} %slice_bitcast_fusion.13), channel_id=1, source_target_pairs={{0,1},{1,2},{2,3},{4,5},{5,6},{6,7},{8,9},{9,10},{10,11},{12,13},{... | collective-permute-start | bytes 24584 | tf_op jit(solution)/shard_map/ppermute | solution.py:26
  114.7 8.1 %fusion.3 = f32[512,64]{1,0:T(8,128)S(1)} fusion(f32[512,64]{1,0:T(8,128)S(1)} %copy.238, bf16[512,64,64]{2,1,0:T(8,128)(2,1)} %gather_fusion, pred[512]{0:T(512)(128)(4,1)S(1)} %compare_and_fusion.1), kind=kLoop, calls=%fused_computation.20 | loop fusion | flops 8355840 | bytes 4456960
  123.1 8.2 %fusion.4 = f32[512,64]{1,0:T(8,128)S(1)} fusion(f32[512,64]{1,0:T(8,128)S(1)} %copy.239, bf16[512,64,64]{2,1,0:T(8,128)(2,1)} %gather_fusion, pred[512]{0:T(512)(128)(4,1)S(1)} %compare_and_fusion.1), kind=kLoop, calls=%fused_computation.21 | loop fusion | flops 8355840 | bytes 4456960
  134.0 3.8 %collective-permute-start.8 = (bf16[1,4,4,256]{3,2,1,0:T(4,128)(2,1)S(1)}, bf16[1,4,4,256]{3,2,1,0:T(4,128)(2,1)S(1)}, u32[]{:S(2)}, u32[]{:S(2)}) collective-permute-start(bf16[1,4,4,256]{3,2,1,0:T(4,128)(2,1)S(1)} %slice_bitcast_fusion.11), channel_id=1, source_target_pairs={{0,1},{1,2},{2,3},{4,5},{5,6},{6,7},{8,9},{9,10},{10,11},{12,13},{... | collective-permute-start | bytes 24584 | tf_op jit(solution)/shard_map/ppermute | solution.py:26
  139.4 3.4 %collective-permute-start.14 = (bf16[64,512]{1,0:T(8,128)(2,1)S(1)}, bf16[64,512]{1,0:T(8,128)(2,1)S(1)}, u32[]{:S(2)}, u32[]{:S(2)}) collective-permute-start(bf16[64,512]{1,0:T(8,128)(2,1)S(1)} %bitcast_convert_fusion), channel_id=1, source_target_pairs={{0,4},{4,8},{8,12},{12,16},{16,20},{20,24},{24,28},{1,5},{5,9},{9,... | collective-permute-start | bytes 196616 | tf_op jit(solution)/shard_map/ppermute | solution.py:38
  144.0 8.4 %fusion.5 = f32[512,64]{1,0:T(8,128)S(1)} fusion(f32[512,64]{1,0:T(8,128)S(1)} %copy.240, bf16[512,64,64]{2,1,0:T(8,128)(2,1)} %gather_fusion, pred[512]{0:T(512)(128)(4,1)S(1)} %compare_and_fusion.1), kind=kLoop, calls=%fused_computation.22 | loop fusion | flops 8355840 | bytes 4456960
  154.9 2.8 %collective-permute-start.10 = (bf16[1,4,4,256]{3,2,1,0:T(4,128)(2,1)S(1)}, bf16[1,4,4,256]{3,2,1,0:T(4,128)(2,1)S(1)}, u32[]{:S(2)}, u32[]{:S(2)}) collective-permute-start(bf16[1,4,4,256]{3,2,1,0:T(4,128)(2,1)S(1)} %slice_bitcast_fusion.9), channel_id=1, source_target_pairs={{0,1},{1,2},{2,3},{4,5},{5,6},{6,7},{8,9},{9,10},{10,11},{12,13},{... | collective-permute-start | bytes 24584 | tf_op jit(solution)/shard_map/ppermute | solution.py:26
  159.5 2.2 collective-permute-done.11
  163.4 8.2 %fusion.6 = f32[512,64]{1,0:T(8,128)S(1)} fusion(f32[512,64]{1,0:T(8,128)S(1)} %copy.241, bf16[512,64,64]{2,1,0:T(8,128)(2,1)} %gather_fusion, pred[512]{0:T(512)(128)(4,1)S(1)} %compare_and_fusion.1), kind=kLoop, calls=%fused_computation.23 | loop fusion | flops 8355840 | bytes 4456960
  174.0 4.3 %collective-permute-start.12 = (bf16[1,4,4,256]{3,2,1,0:T(4,128)(2,1)S(1)}, bf16[1,4,4,256]{3,2,1,0:T(4,128)(2,1)S(1)}, u32[]{:S(2)}, u32[]{:S(2)}) collective-permute-start(bf16[1,4,4,256]{3,2,1,0:T(4,128)(2,1)S(1)} %slice_bitcast_fusion.7), channel_id=1, source_target_pairs={{0,1},{1,2},{2,3},{4,5},{5,6},{6,7},{8,9},{9,10},{10,11},{12,13},{... | collective-permute-start | bytes 24584 | tf_op jit(solution)/shard_map/ppermute | solution.py:26
  183.8 8.2 %fusion.7 = f32[512,64]{1,0:T(8,128)S(1)} fusion(f32[512,64]{1,0:T(8,128)S(1)} %copy.242, bf16[512,64,64]{2,1,0:T(8,128)(2,1)} %gather_fusion, pred[512]{0:T(512)(128)(4,1)S(1)} %compare_and_fusion.1), kind=kLoop, calls=%fused_computation.24 | loop fusion | flops 8355840 | bytes 4456960
  194.5 3.0 %collective-permute-start.15 = (bf16[1,4,4,256]{3,2,1,0:T(4,128)(2,1)S(1)}, bf16[1,4,4,256]{3,2,1,0:T(4,128)(2,1)S(1)}, u32[]{:S(2)}, u32[]{:S(2)}) collective-permute-start(bf16[1,4,4,256]{3,2,1,0:T(4,128)(2,1)S(1)} %slice_bitcast_fusion.5), channel_id=1, source_target_pairs={{0,1},{1,2},{2,3},{4,5},{5,6},{6,7},{8,9},{9,10},{10,11},{12,13},{... | collective-permute-start | bytes 24584 | tf_op jit(solution)/shard_map/ppermute | solution.py:26
  211.1 41.3 %all-reduce.8 = f32[32]{0:T(128)S(1)} all-reduce(f32[32]{0:T(128)S(1)} %dynamic-update-slice.144), channel_id=1, replica_groups=mesh['tm'=8,'space'=4] {'tm','space'}, use_global_device_ids=true, to_apply=%add.8 | all-reduce | flops 32 | bytes 256
  258.1 5.1 %collective-permute-done.17 = f32[64,512]{0,1:T(8,128)S(1)} collective-permute-done((f32[64,512]{0,1:T(8,128)S(1)}, f32[64,512]{0,1:T(8,128)S(1)}, u32[]{:S(2)}, u32[]{:S(2)}) %collective-permute-start.17) | collective-permute-done | bytes 131104 | tf_op jit(solution)/shard_map/ppermute | solution.py:38
  (480 shorter events, 65.5 us)
Async XLA Ops:
  0.6 11.7 %copy-start.3 = (s32[1,512]{1,0:T(1,128)S(1)}, s32[1,512]{1,0:T(1,128)}, u32[]{:S(2)}) copy-start(s32[1,512]{1,0:T(1,128)} %param.111) | copy-start | bytes 6148
  0.6 11.9 %copy-start = (bf16[4,64,512]{2,1,0:T(8,128)(2,1)S(1)}, bf16[4,64,512]{2,1,0:T(8,128)(2,1)}, u32[]{:S(2)}) copy-start(bf16[4,64,512]{2,1,0:T(8,128)(2,1)} %param.106) | copy-start | bytes 786436
  6.1 48.6 %collective-permute-start = (bf16[1,4,4,256]{3,2,1,0:T(4,128)(2,1)S(1)}, bf16[1,4,4,256]{3,2,1,0:T(4,128)(2,1)S(1)}, u32[]{:S(2)}, u32[]{:S(2)}) collective-permute-start(bf16[1,4,4,256]{3,2,1,0:T(4,128)(2,1)S(1)} %slice_bitcast_fusion.19), channel_id=1, source_target_pairs={{0,1},{1,2},{2,3},{4,5},{5,6},{6,7},{8,9},{9,10},{10,11},{12,13},{... | collective-permute-start | bytes 24584 | tf_op jit(solution)/shard_map/ppermute | solution.py:26
  8.6 46.2 %collective-permute-start.1 = (bf16[1,4,4,256]{3,2,1,0:T(4,128)(2,1)S(1)}, bf16[1,4,4,256]{3,2,1,0:T(4,128)(2,1)S(1)}, u32[]{:S(2)}, u32[]{:S(2)}) collective-permute-start(bf16[1,4,4,256]{3,2,1,0:T(4,128)(2,1)S(1)} %slice_bitcast_fusion.18), channel_id=1, source_target_pairs={{1,0},{2,1},{3,2},{5,4},{6,5},{7,6},{9,8},{10,9},{11,10},{13,12},{... | collective-permute-start | bytes 24584 | tf_op jit(solution)/shard_map/ppermute | solution.py:28
  15.7 36.1 %copy-start.2 = (bf16[64,512]{1,0:T(8,128)(2,1)S(1)}, bf16[64,512]{1,0:T(8,128)(2,1)}, u32[]{:S(2)}) copy-start(bf16[64,512]{1,0:T(8,128)(2,1)} %param.107) | copy-start | bytes 196612
  15.7 37.7 %copy-start.1 = (f32[1,64,512]{2,1,0:T(8,128)S(1)}, f32[1,64,512]{2,1,0:T(8,128)}, u32[]{:S(2)}) copy-start(f32[1,64,512]{2,1,0:T(8,128)} %param.109) | copy-start | bytes 393220
  66.5 7.1 %collective-permute-start.2 = (bf16[1,4,4,256]{3,2,1,0:T(4,128)(2,1)S(1)}, bf16[1,4,4,256]{3,2,1,0:T(4,128)(2,1)S(1)}, u32[]{:S(2)}, u32[]{:S(2)}) collective-permute-start(bf16[1,4,4,256]{3,2,1,0:T(4,128)(2,1)S(1)} %slice_bitcast_fusion.17), channel_id=1, source_target_pairs={{0,1},{1,2},{2,3},{4,5},{5,6},{6,7},{8,9},{9,10},{10,11},{12,13},{... | collective-permute-start | bytes 24584 | tf_op jit(solution)/shard_map/ppermute | solution.py:26
  71.7 4.3 %collective-permute-start.3 = (bf16[1,4,4,256]{3,2,1,0:T(4,128)(2,1)S(1)}, bf16[1,4,4,256]{3,2,1,0:T(4,128)(2,1)S(1)}, u32[]{:S(2)}, u32[]{:S(2)}) collective-permute-start(bf16[1,4,4,256]{3,2,1,0:T(4,128)(2,1)S(1)} %slice_bitcast_fusion.16), channel_id=1, source_target_pairs={{1,0},{2,1},{3,2},{5,4},{6,5},{7,6},{9,8},{10,9},{11,10},{13,12},{... | collective-permute-start | bytes 24584 | tf_op jit(solution)/shard_map/ppermute | solution.py:28
  87.5 6.2 %collective-permute-start.4 = (bf16[1,4,4,256]{3,2,1,0:T(4,128)(2,1)S(1)}, bf16[1,4,4,256]{3,2,1,0:T(4,128)(2,1)S(1)}, u32[]{:S(2)}, u32[]{:S(2)}) collective-permute-start(bf16[1,4,4,256]{3,2,1,0:T(4,128)(2,1)S(1)} %slice_bitcast_fusion.15), channel_id=1, source_target_pairs={{0,1},{1,2},{2,3},{4,5},{5,6},{6,7},{8,9},{9,10},{10,11},{12,13},{... | collective-permute-start | bytes 24584 | tf_op jit(solution)/shard_map/ppermute | solution.py:26
  91.8 3.1 %collective-permute-start.5 = (bf16[1,4,4,256]{3,2,1,0:T(4,128)(2,1)S(1)}, bf16[1,4,4,256]{3,2,1,0:T(4,128)(2,1)S(1)}, u32[]{:S(2)}, u32[]{:S(2)}) collective-permute-start(bf16[1,4,4,256]{3,2,1,0:T(4,128)(2,1)S(1)} %slice_bitcast_fusion.14), channel_id=1, source_target_pairs={{1,0},{2,1},{3,2},{5,4},{6,5},{7,6},{9,8},{10,9},{11,10},{13,12},{... | collective-permute-start | bytes 24584 | tf_op jit(solution)/shard_map/ppermute | solution.py:28
  106.8 5.8 %collective-permute-start.6 = (bf16[1,4,4,256]{3,2,1,0:T(4,128)(2,1)S(1)}, bf16[1,4,4,256]{3,2,1,0:T(4,128)(2,1)S(1)}, u32[]{:S(2)}, u32[]{:S(2)}) collective-permute-start(bf16[1,4,4,256]{3,2,1,0:T(4,128)(2,1)S(1)} %slice_bitcast_fusion.13), channel_id=1, source_target_pairs={{0,1},{1,2},{2,3},{4,5},{5,6},{6,7},{8,9},{9,10},{10,11},{12,13},{... | collective-permute-start | bytes 24584 | tf_op jit(solution)/shard_map/ppermute | solution.py:26
  110.7 3.1 %collective-permute-start.7 = (bf16[1,4,4,256]{3,2,1,0:T(4,128)(2,1)S(1)}, bf16[1,4,4,256]{3,2,1,0:T(4,128)(2,1)S(1)}, u32[]{:S(2)}, u32[]{:S(2)}) collective-permute-start(bf16[1,4,4,256]{3,2,1,0:T(4,128)(2,1)S(1)} %slice_bitcast_fusion.12), channel_id=1, source_target_pairs={{1,0},{2,1},{3,2},{5,4},{6,5},{7,6},{9,8},{10,9},{11,10},{13,12},{... | collective-permute-start | bytes 24584 | tf_op jit(solution)/shard_map/ppermute | solution.py:28
  134.0 9.0 %collective-permute-start.8 = (bf16[1,4,4,256]{3,2,1,0:T(4,128)(2,1)S(1)}, bf16[1,4,4,256]{3,2,1,0:T(4,128)(2,1)S(1)}, u32[]{:S(2)}, u32[]{:S(2)}) collective-permute-start(bf16[1,4,4,256]{3,2,1,0:T(4,128)(2,1)S(1)} %slice_bitcast_fusion.11), channel_id=1, source_target_pairs={{0,1},{1,2},{2,3},{4,5},{5,6},{6,7},{8,9},{9,10},{10,11},{12,13},{... | collective-permute-start | bytes 24584 | tf_op jit(solution)/shard_map/ppermute | solution.py:26
  137.9 5.2 %collective-permute-start.9 = (bf16[1,4,4,256]{3,2,1,0:T(4,128)(2,1)S(1)}, bf16[1,4,4,256]{3,2,1,0:T(4,128)(2,1)S(1)}, u32[]{:S(2)}, u32[]{:S(2)}) collective-permute-start(bf16[1,4,4,256]{3,2,1,0:T(4,128)(2,1)S(1)} %slice_bitcast_fusion.10), channel_id=1, source_target_pairs={{1,0},{2,1},{3,2},{5,4},{6,5},{7,6},{9,8},{10,9},{11,10},{13,12},{... | collective-permute-start | bytes 24584 | tf_op jit(solution)/shard_map/ppermute | solution.py:28
  139.4 116.6 %collective-permute-start.14 = (bf16[64,512]{1,0:T(8,128)(2,1)S(1)}, bf16[64,512]{1,0:T(8,128)(2,1)S(1)}, u32[]{:S(2)}, u32[]{:S(2)}) collective-permute-start(bf16[64,512]{1,0:T(8,128)(2,1)S(1)} %bitcast_convert_fusion), channel_id=1, source_target_pairs={{0,4},{4,8},{8,12},{12,16},{16,20},{20,24},{24,28},{1,5},{5,9},{9,... | collective-permute-start | bytes 196616 | tf_op jit(solution)/shard_map/ppermute | solution.py:38
  154.9 4.7 %collective-permute-start.10 = (bf16[1,4,4,256]{3,2,1,0:T(4,128)(2,1)S(1)}, bf16[1,4,4,256]{3,2,1,0:T(4,128)(2,1)S(1)}, u32[]{:S(2)}, u32[]{:S(2)}) collective-permute-start(bf16[1,4,4,256]{3,2,1,0:T(4,128)(2,1)S(1)} %slice_bitcast_fusion.9), channel_id=1, source_target_pairs={{0,1},{1,2},{2,3},{4,5},{5,6},{6,7},{8,9},{9,10},{10,11},{12,13},{... | collective-permute-start | bytes 24584 | tf_op jit(solution)/shard_map/ppermute | solution.py:26
  157.6 4.1 %collective-permute-start.11 = (bf16[1,4,4,256]{3,2,1,0:T(4,128)(2,1)S(1)}, bf16[1,4,4,256]{3,2,1,0:T(4,128)(2,1)S(1)}, u32[]{:S(2)}, u32[]{:S(2)}) collective-permute-start(bf16[1,4,4,256]{3,2,1,0:T(4,128)(2,1)S(1)} %slice_bitcast_fusion.8), channel_id=1, source_target_pairs={{1,0},{2,1},{3,2},{5,4},{6,5},{7,6},{9,8},{10,9},{11,10},{13,12},{... | collective-permute-start | bytes 24584 | tf_op jit(solution)/shard_map/ppermute | solution.py:28
  174.0 8.8 %collective-permute-start.12 = (bf16[1,4,4,256]{3,2,1,0:T(4,128)(2,1)S(1)}, bf16[1,4,4,256]{3,2,1,0:T(4,128)(2,1)S(1)}, u32[]{:S(2)}, u32[]{:S(2)}) collective-permute-start(bf16[1,4,4,256]{3,2,1,0:T(4,128)(2,1)S(1)} %slice_bitcast_fusion.7), channel_id=1, source_target_pairs={{0,1},{1,2},{2,3},{4,5},{5,6},{6,7},{8,9},{9,10},{10,11},{12,13},{... | collective-permute-start | bytes 24584 | tf_op jit(solution)/shard_map/ppermute | solution.py:26
  178.4 4.5 %collective-permute-start.13 = (bf16[1,4,4,256]{3,2,1,0:T(4,128)(2,1)S(1)}, bf16[1,4,4,256]{3,2,1,0:T(4,128)(2,1)S(1)}, u32[]{:S(2)}, u32[]{:S(2)}) collective-permute-start(bf16[1,4,4,256]{3,2,1,0:T(4,128)(2,1)S(1)} %slice_bitcast_fusion.6), channel_id=1, source_target_pairs={{1,0},{2,1},{3,2},{5,4},{6,5},{7,6},{9,8},{10,9},{11,10},{13,12},{... | collective-permute-start | bytes 24584 | tf_op jit(solution)/shard_map/ppermute | solution.py:28
  194.5 5.2 %collective-permute-start.15 = (bf16[1,4,4,256]{3,2,1,0:T(4,128)(2,1)S(1)}, bf16[1,4,4,256]{3,2,1,0:T(4,128)(2,1)S(1)}, u32[]{:S(2)}, u32[]{:S(2)}) collective-permute-start(bf16[1,4,4,256]{3,2,1,0:T(4,128)(2,1)S(1)} %slice_bitcast_fusion.5), channel_id=1, source_target_pairs={{0,1},{1,2},{2,3},{4,5},{5,6},{6,7},{8,9},{9,10},{10,11},{12,13},{... | collective-permute-start | bytes 24584 | tf_op jit(solution)/shard_map/ppermute | solution.py:26
  197.6 3.8 %collective-permute-start.16 = (bf16[1,4,4,256]{3,2,1,0:T(4,128)(2,1)S(1)}, bf16[1,4,4,256]{3,2,1,0:T(4,128)(2,1)S(1)}, u32[]{:S(2)}, u32[]{:S(2)}) collective-permute-start(bf16[1,4,4,256]{3,2,1,0:T(4,128)(2,1)S(1)} %slice_bitcast_fusion.4), channel_id=1, source_target_pairs={{1,0},{2,1},{3,2},{5,4},{6,5},{7,6},{9,8},{10,9},{11,10},{13,12},{... | collective-permute-start | bytes 24584 | tf_op jit(solution)/shard_map/ppermute | solution.py:28
  254.1 9.1 %collective-permute-start.17 = (f32[64,512]{0,1:T(8,128)S(1)}, f32[64,512]{0,1:T(8,128)S(1)}, u32[]{:S(2)}, u32[]{:S(2)}) collective-permute-start(f32[64,512]{0,1:T(8,128)S(1)} %select_bitcast_fusion.1), channel_id=1, source_target_pairs={{4,0},{8,4},{12,8},{16,12},{20,16},{24,20},{28,24},{5,1},{9,5},{13... | collective-permute-start | bytes 393224 | tf_op jit(solution)/shard_map/ppermute | solution.py:38
